TPU v7x, 512 devices: a whole 4x8x8 slice. The times are simulated.
512 devices in a mesh: dp: 8 (over z), expert: 64 (over y, x, core).
Axes of the slice: x: 4, y: 8, z: 8, core: 2. Of those that a mesh axis runs over, the one named last changes fastest.
Arguments:
- tokens: bfloat16 [65536, 3584], P(('dp', 'expert')), may hold values from -6 to 6
- cotangent: bfloat16 [65536, 3584], P(('dp', 'expert')), may hold values from -6 to 6
- route_ids: int32 [65536, 8], P(('dp', 'expert')), may hold values from 0 to 255, as said below
- route_gates: float32 [65536, 8], P(('dp', 'expert')), may hold values from 0.1 to 1
- gate_w: bfloat16 [3584, 8192], P('dp', 'expert'), may hold values from -0.09375 to 0.09375
- up_w: bfloat16 [3584, 8192], P('dp', 'expert'), may hold values from -0.09375 to 0.09375
- down_w: bfloat16 [3584, 8192], P('dp', 'expert'), may hold values from -0.1875 to 0.1875
Outputs:
- moe_out: bfloat16 [65536, 3584], P(('dp', 'expert'))
- d_tokens: bfloat16 [65536, 3584], P(('dp', 'expert'))
- d_gates: float32 [65536, 8], P(('dp', 'expert'))
- d_gate_w: bfloat16 [3584, 8192], P('dp', 'expert')
- d_up_w: bfloat16 [3584, 8192], P('dp', 'expert')
- d_down_w: bfloat16 [3584, 8192], P('dp', 'expert')
Inputs may be any that keep to these rules, and one draw needn't show every extreme that they name: `route_ids`: each token names 8 different experts; the experts in flight are 0 to 7. Among the tokens of one device (aligned blocks of 128 tokens) each expert in flight is named by at most 6 tokens, and in every draw one expert in flight is named by exactly 6 tokens in every block.
All inputs are finite; a program needn't handle non-finite values.
Results may differ from a plain program's by a relative error of at most 0.017.
Values may be sent and summed in bfloat16 or wider, within the bound.
A program may use at most 64 MiB of HBM per device.

v0:
```python
import jax
import jax.numpy as jnp
from jax import lax
from jax.sharding import PartitionSpec as P

TOP = 8
SLICES = 8
CAP = 6


def shards(tokens, cotangent, route_ids, route_gates, gate_w, up_w, down_w):
    owners = lax.axis_size("expert")
    groups = owners // SLICES
    tok_rows = tokens.shape[0]
    routes = tok_rows * TOP
    flat_ids = route_ids.reshape(routes)
    matched = (flat_ids[:, None] == jnp.arange(groups, dtype=jnp.int32)[None, :]).astype(jnp.int32)
    slot_index = jnp.cumsum(matched, axis=0) - 1
    chosen = (matched[:, :, None] == 1) & (
        slot_index[:, :, None] == jnp.arange(CAP, dtype=jnp.int32)[None, None, :]
    )
    select = jnp.transpose(chosen, (1, 2, 0)).reshape(groups * CAP, routes).astype(jnp.float32)
    tok_select = jnp.sum(select.reshape(groups * CAP, tok_rows, TOP), axis=2)
    slot_gate = jnp.sum(select * route_gates.reshape(routes)[None, :], axis=1)
    pick_rows = tok_select.astype(jnp.bfloat16)
    token_slots = jnp.dot(pick_rows, tokens, preferred_element_type=jnp.float32).astype(
        jnp.bfloat16
    )
    cotangent_slots = jnp.dot(pick_rows, cotangent, preferred_element_type=jnp.float32).astype(
        jnp.bfloat16
    )
    scaled_slots = (slot_gate[:, None] * cotangent_slots.astype(jnp.float32)).astype(jnp.bfloat16)

    def spread(slot_rows):
        width = slot_rows.shape[1]
        grouped = slot_rows.reshape(groups, 1, CAP, width)
        return jnp.broadcast_to(grouped, (groups, SLICES, CAP, width)).reshape(owners * CAP, width)

    w_gate, w_up, w_down = (
        lax.all_gather(gate_w, "dp", axis=0, tiled=True),
        lax.all_gather(up_w, "dp", axis=0, tiled=True),
        lax.all_gather(down_w, "dp", axis=0, tiled=True),
    )
    token_rows = lax.all_to_all(
        spread(token_slots), "expert", split_axis=0, concat_axis=0, tiled=True
    )
    gate_pre = jnp.dot(token_rows, w_gate, preferred_element_type=jnp.float32)
    up_pre = jnp.dot(token_rows, w_up, preferred_element_type=jnp.float32)
    sigmoid_gate = jax.nn.sigmoid(gate_pre)
    active = gate_pre * sigmoid_gate
    hidden = (active * up_pre).astype(jnp.bfloat16)
    contract_cols = (((1,), (1,)), ((), ()))
    out_part = lax.dot_general(
        hidden, w_down, contract_cols, preferred_element_type=jnp.float32
    ).astype(jnp.bfloat16)
    out_back = lax.all_to_all(out_part, "expert", split_axis=0, concat_axis=0, tiled=True)
    scaled_rows = lax.all_to_all(
        spread(scaled_slots), "expert", split_axis=0, concat_axis=0, tiled=True
    )
    d_hidden = jnp.dot(scaled_rows, w_down, preferred_element_type=jnp.float32)
    d_gate_pre = (
        d_hidden * up_pre * sigmoid_gate * (1.0 + gate_pre * (1.0 - sigmoid_gate))
    ).astype(jnp.bfloat16)
    d_up_pre = (d_hidden * active).astype(jnp.bfloat16)
    dx_part = lax.dot_general(d_gate_pre, w_gate, contract_cols, preferred_element_type=jnp.float32)
    dx_part = (
        dx_part + lax.dot_general(d_up_pre, w_up, contract_cols, preferred_element_type=jnp.float32)
    ).astype(jnp.bfloat16)
    contract_rows = (((0,), (0,)), ((), ()))
    gate_term = lax.dot_general(
        token_rows, d_gate_pre, contract_rows, preferred_element_type=jnp.float32
    )
    up_term = lax.dot_general(
        token_rows, d_up_pre, contract_rows, preferred_element_type=jnp.float32
    )
    down_term = lax.dot_general(
        scaled_rows, hidden, contract_rows, preferred_element_type=jnp.float32
    )
    summed_grads = lax.psum_scatter(
        jnp.concatenate([gate_term, up_term, down_term], axis=1).astype(jnp.bfloat16),
        "dp",
        scatter_dimension=0,
        tiled=True,
    ).astype(jnp.float32)
    hidden_cols = gate_w.shape[1]
    d_gate_w = summed_grads[:, :hidden_cols].astype(jnp.bfloat16)
    d_up_w = summed_grads[:, hidden_cols : 2 * hidden_cols].astype(jnp.bfloat16)
    d_down_w = summed_grads[:, 2 * hidden_cols :].astype(jnp.bfloat16)
    dx_back = lax.all_to_all(dx_part, "expert", split_axis=0, concat_axis=0, tiled=True)
    member_wide = spread(tok_select)
    weighted_wide = spread(tok_select * slot_gate[:, None])
    weight_high = weighted_wide.astype(jnp.bfloat16)
    weight_low = (weighted_wide - weight_high.astype(jnp.float32)).astype(jnp.bfloat16)
    moe_sum = lax.dot_general(
        weight_high, out_back, contract_rows, preferred_element_type=jnp.float32
    )
    moe_sum = moe_sum + lax.dot_general(
        weight_low, out_back, contract_rows, preferred_element_type=jnp.float32
    )
    moe_out = moe_sum.astype(jnp.bfloat16)
    d_tokens = lax.dot_general(
        member_wide.astype(jnp.bfloat16), dx_back, contract_rows, preferred_element_type=jnp.float32
    ).astype(jnp.bfloat16)
    inner = lax.dot_general(cotangent, out_back, contract_cols, preferred_element_type=jnp.float32)
    wide_grad = jnp.sum(inner * jnp.transpose(member_wide), axis=0)
    slot_grad = jnp.sum(wide_grad.reshape(groups, SLICES, CAP), axis=1).reshape(groups * CAP)
    d_gates = jnp.sum(slot_grad[:, None] * select, axis=0).reshape(tok_rows, TOP)
    return (moe_out, d_tokens, d_gates, d_gate_w, d_up_w, d_down_w)


def solution(mesh):
    return jax.shard_map(
        shards,
        mesh=mesh,
        in_specs=(
            P(("dp", "expert"), None),
            P(("dp", "expert"), None),
            P(("dp", "expert"), None),
            P(("dp", "expert"), None),
            P("dp", "expert"),
            P("dp", "expert"),
            P("dp", "expert"),
        ),
        out_specs=(
            P(("dp", "expert"), None),
            P(("dp", "expert"), None),
            P(("dp", "expert"), None),
            P("dp", "expert"),
            P("dp", "expert"),
            P("dp", "expert"),
        ),
        check_vma=False,
    )
```

profile of v0, /device:TPU:2, one launch (start us, length us, event | category | flops | bytes accessed | tf_op | source)
XLA Modules:
  0.0 461.1 jit_solution(1026153735217437292)
XLA Ops:
  7.2 0.0 copy-start
  7.2 0.9 copy.27
  8.1 0.1 eq.76
  8.1 0.1 eq.70
  8.2 0.1 eq.83
  8.4 2.3 reduce-window.6
  10.6 0.3 slice_reduce_fusion
  10.9 0.2 reduce-window.9
  11.1 0.1 add_bitcast_fusion
  11.2 1.9 and.18
  13.2 3.4 eq.81
  16.6 2.9 convert_reduce_fusion
  19.6 0.3 convolution_convert_fusion.6
  19.8 0.1 broadcast_in_dim.17
  19.9 2.1 broadcast_in_dim.36
  22.1 11.0 %all-to-all-start = ((bf16[64,6,3584]{2,1,0:T(8,128)(2,1)}), bf16[64,6,3584]{2,1,0:T(8,128)(2,1)}, u32[]{:S(2)}, u32[]{:S(2)}) async-start(bf16[64,6,3584]{2,1,0:T(8,128)(2,1)} %bitcast.37), calls=%async_computation | async-start | bytes 7340032 | tf_op jit(solution)/shard_map/all_to_all | solution.py:44
  33.1 32.2 %all_gather.9 = bf16[3584,128]{1,0:T(8,128)(2,1)S(1)} all-gather(bf16[448,128]{1,0:T(8,128)(2,1)S(1)} %copy-done.10), channel_id=1, replica_groups=mesh['dp'=8,'expert'=64] {'dp'}, dimensions={0}, use_global_device_ids=true | all-gather | bytes 1032192 | tf_op jit(solution)/shard_map/all_gather | solution.py:40
  65.3 26.5 %all_gather.10 = bf16[3584,128]{1,0:T(8,128)(2,1)S(1)} all-gather(bf16[448,128]{1,0:T(8,128)(2,1)S(1)} %copy-done.11), channel_id=1, replica_groups=mesh['dp'=8,'expert'=64] {'dp'}, dimensions={0}, use_global_device_ids=true | all-gather | bytes 1032192 | tf_op jit(solution)/shard_map/all_gather | solution.py:41
  91.8 28.6 %all_gather.11 = bf16[3584,128]{1,0:T(8,128)(2,1)} all-gather(bf16[448,128]{1,0:T(8,128)(2,1)S(1)} %copy-done.12), channel_id=1, replica_groups=mesh['dp'=8,'expert'=64] {'dp'}, dimensions={0}, use_global_device_ids=true | all-gather | bytes 1032192 | tf_op jit(solution)/shard_map/all_gather | solution.py:42
  120.4 5.5 %all_to_all.34 = bf16[384,3584]{1,0:T(8,128)(2,1)} reshape(bf16[64,6,3584]{2,1,0:T(8,128)(2,1)} %all-to-all-done) | data formatting | bytes 5505024 | tf_op jit(solution)/shard_map/all_to_all | solution.py:44
  125.8 2.8 fusion.12
  128.7 0.9 multiply_convert_fusion.2
  129.6 0.3 copy-done.7
  129.8 2.5 convolution_convert_fusion
  132.3 5.4 %all_to_all.35 = bf16[64,6,3584]{2,1,0:T(8,128)(2,1)} reshape(bf16[384,3584]{1,0:T(8,128)(2,1)} %convolution_convert_fusion) | data formatting | bytes 5505024 | tf_op jit(solution)/shard_map/all_to_all | solution.py:56
  137.7 10.1 %all-to-all-start.1 = ((bf16[64,6,3584]{2,1,0:T(8,128)(2,1)}), bf16[64,6,3584]{2,1,0:T(8,128)(2,1)}, u32[]{:S(2)}, u32[]{:S(2)}) async-start(bf16[64,6,3584]{2,1,0:T(8,128)(2,1)} %all_to_all.35), calls=%async_computation.1 | async-start | bytes 7340032 | tf_op jit(solution)/shard_map/all_to_all | solution.py:56
  147.9 0.1 copy.29
  148.0 0.1 mul.65
  148.1 0.1 copy.30
  148.2 84.5 %all-to-all-done.1 = bf16[64,6,3584]{2,1,0:T(8,128)(2,1)} async-done(((bf16[64,6,3584]{2,1,0:T(8,128)(2,1)}), bf16[64,6,3584]{2,1,0:T(8,128)(2,1)}, u32[]{:S(2)}, u32[]{:S(2)}) %all-to-all-start.1) | async-done | bytes 2752544 | tf_op jit(solution)/shard_map/all_to_all | solution.py:56
  232.7 5.5 %all_to_all.37 = bf16[384,3584]{1,0:T(8,128)(2,1)} reshape(bf16[64,6,3584]{2,1,0:T(8,128)(2,1)} %all-to-all-done.1) | data formatting | bytes 5505024 | tf_op jit(solution)/shard_map/all_to_all | solution.py:56
  238.2 2.7 fusion.5
  241.0 0.1 reshape.139
  241.2 0.2 select_reduce_fusion
  241.3 0.1 mul.72
  241.4 0.3 fusion.4
  241.7 0.1 broadcast_in_dim.39
  241.8 0.3 broadcast_in_dim.40
  242.1 90.3 %all_to_all.48 = bf16[64,6,3584]{2,1,0:T(8,128)(2,1)} all-to-all(bf16[64,6,3584]{2,1,0:T(8,128)(2,1)S(1)} %bitcast.38), channel_id=1, replica_groups=mesh['dp'=8,'expert'=64] {'expert'}, dimensions={0} | all-to-all | bytes 5505024 | tf_op jit(solution)/shard_map/all_to_all | solution.py:57
  332.4 5.5 %all_to_all.40 = bf16[384,3584]{1,0:T(8,128)(2,1)} reshape(bf16[64,6,3584]{2,1,0:T(8,128)(2,1)} %all_to_all.48) | data formatting | bytes 5505024 | tf_op jit(solution)/shard_map/all_to_all | solution.py:57
  337.9 2.6 convolution_convert_fusion.1
  340.5 0.2 copy-done.8
  340.7 0.9 multiply_convert_fusion
  341.6 0.9 copy-done.3
  342.5 0.7 convolution_convert_fusion.3
  343.2 0.9 fusion.14
  344.1 0.7 convolution_convert_fusion.2
  344.8 0.5 copy-done.6
  345.2 2.4 fusion
  347.7 5.4 %all_to_all.41 = bf16[64,6,3584]{2,1,0:T(8,128)(2,1)} reshape(bf16[384,3584]{1,0:T(8,128)(2,1)} %fusion) | data formatting | bytes 5505024 | tf_op jit(solution)/shard_map/all_to_all | solution.py:89
  353.1 5.6 %all-to-all-start.3 = ((bf16[64,6,3584]{2,1,0:T(8,128)(2,1)}), bf16[64,6,3584]{2,1,0:T(8,128)(2,1)}, u32[]{:S(2)}, u32[]{:S(2)}) async-start(bf16[64,6,3584]{2,1,0:T(8,128)(2,1)} %all_to_all.41), calls=%async_computation.3 | async-start | bytes 7340032 | tf_op jit(solution)/shard_map/all_to_all | solution.py:89
  358.7 0.0 reduce-scatter.4.cloned.1.call-start
  358.7 1.7 pad_maximum_fusion
  360.4 4.5 copy.35
  364.9 0.0 reduce-scatter.4.cloned.1.call-update
  365.0 0.1 reshape.140
  365.0 0.7 copy.31
  365.7 0.1 subtract_convert_fusion
  366.0 2.4 fusion.13
  368.5 3.4 fusion.1
  371.8 71.8 %all-to-all-done.3 = bf16[64,6,3584]{2,1,0:T(8,128)(2,1)} async-done(((bf16[64,6,3584]{2,1,0:T(8,128)(2,1)}), bf16[64,6,3584]{2,1,0:T(8,128)(2,1)}, u32[]{:S(2)}, u32[]{:S(2)}) %all-to-all-start.3) | async-done | bytes 2752544 | tf_op jit(solution)/shard_map/all_to_all | solution.py:89
  443.6 5.6 %all_to_all.43 = bf16[384,3584]{1,0:T(8,128)(2,1)} reshape(bf16[64,6,3584]{2,1,0:T(8,128)(2,1)} %all-to-all-done.3) | data formatting | bytes 5505024 | tf_op jit(solution)/shard_map/all_to_all | solution.py:89
  449.2 3.4 convolution_convert_fusion.4
  452.6 1.7 fusion.11
  (41 shorter events, 0.4 us)
Async XLA Ops:
  7.2 231.1 %copy-start = (bf16[128,3584]{1,0:T(8,128)(2,1)S(1)}, bf16[128,3584]{1,0:T(8,128)(2,1)}, u32[]{:S(2)}) copy-start(bf16[128,3584]{1,0:T(8,128)(2,1)} %param.8) | copy-start | bytes 2752516
  16.6 2.9 copy-start.9
  22.0 11.0 %copy-start.10 = (bf16[448,128]{1,0:T(8,128)(2,1)S(1)}, bf16[448,128]{1,0:T(8,128)(2,1)}, u32[]{:S(2)}) copy-start(bf16[448,128]{1,0:T(8,128)(2,1)} %param.11) | copy-start | bytes 344068
  22.0 43.2 %copy-start.11 = (bf16[448,128]{1,0:T(8,128)(2,1)S(1)}, bf16[448,128]{1,0:T(8,128)(2,1)}, u32[]{:S(2)}) copy-start(bf16[448,128]{1,0:T(8,128)(2,1)} %param.12) | copy-start | bytes 344068
  22.1 69.8 %copy-start.12 = (bf16[448,128]{1,0:T(8,128)(2,1)S(1)}, bf16[448,128]{1,0:T(8,128)(2,1)}, u32[]{:S(2)}) copy-start(bf16[448,128]{1,0:T(8,128)(2,1)} %param.13) | copy-start | bytes 344068
  22.1 98.3 %all-to-all-start = ((bf16[64,6,3584]{2,1,0:T(8,128)(2,1)}), bf16[64,6,3584]{2,1,0:T(8,128)(2,1)}, u32[]{:S(2)}, u32[]{:S(2)}) async-start(bf16[64,6,3584]{2,1,0:T(8,128)(2,1)} %bitcast.37), calls=%async_computation | async-start | bytes 7340032 | tf_op jit(solution)/shard_map/all_to_all | solution.py:44
  91.8 36.8 %copy-start.5 = (bf16[3584,128]{1,0:T(8,128)(2,1)}, bf16[3584,128]{1,0:T(8,128)(2,1)S(1)}, u32[]{:S(2)}) copy-start(bf16[3584,128]{1,0:T(8,128)(2,1)S(1)} %all_gather.10) | copy-start | bytes 2752516
  125.8 2.8 copy-start.2
  128.7 1.2 copy-start.7
  137.7 10.1 %copy-start.13 = (f32[128,8]{0,1:T(8,128)S(1)}, f32[128,8]{0,1:T(8,128)}, u32[]{:S(2)}) copy-start(f32[128,8]{0,1:T(8,128)} %param.10) | copy-start | bytes 12292
  137.7 95.0 %all-to-all-start.1 = ((bf16[64,6,3584]{2,1,0:T(8,128)(2,1)}), bf16[64,6,3584]{2,1,0:T(8,128)(2,1)}, u32[]{:S(2)}, u32[]{:S(2)}) async-start(bf16[64,6,3584]{2,1,0:T(8,128)(2,1)} %all_to_all.35), calls=%async_computation.1 | async-start | bytes 7340032 | tf_op jit(solution)/shard_map/all_to_all | solution.py:56
  337.8 2.6 copy-start.4
  337.9 2.8 copy-start.8
  340.7 1.8 copy-start.3
  344.0 1.2 copy-start.6
  353.1 90.6 %all-to-all-start.3 = ((bf16[64,6,3584]{2,1,0:T(8,128)(2,1)}), bf16[64,6,3584]{2,1,0:T(8,128)(2,1)}, u32[]{:S(2)}, u32[]{:S(2)}) async-start(bf16[64,6,3584]{2,1,0:T(8,128)(2,1)} %all_to_all.41), calls=%async_computation.3 | async-start | bytes 7340032 | tf_op jit(solution)/shard_map/all_to_all | solution.py:89
  358.7 93.9 %reduce-scatter.4.cloned.1.call-start = ((), (), s32[]{:S(2)}) async-start(), calls=%async_computation.5 | async-start | bytes 3096576
  443.6 10.7 %copy-start.1 = (bf16[128,3584]{1,0:T(8,128)(2,1)S(1)}, bf16[128,3584]{1,0:T(8,128)(2,1)}, u32[]{:S(2)}) copy-start(bf16[128,3584]{1,0:T(8,128)(2,1)} %param.8) | copy-start | bytes 2752516
Sparse Core Ops, SparseCore 0:
  365.1 46.6 reduce-scatter.3
where the time goes:
time: 463 us; the launch traced here: 461 us
  blocking collectives  178 us (38%)
  waiting for transfers between devices  156 us (34%)
  local copies, waits for them, and re-layouts  51.9 us (11%)
  matrix products  26.8 us (6%)
  starting transfers between devices  26.8 us (6%)
  between operations  14.4 us (3%)
  other arithmetic  7.41 us (2%)
    all_to_all x1, blocking collectives, shards(): lax.all_to_all(spread(scaled_slots), 'expert', split_axis=0, concat_axis=...  90.3 us
    all_to_all x1, waiting for transfers between devices, shards(): lax.all_to_all(out_part, 'expert', split_axis=0, concat_axis=0, tiled=True)  84.5 us
    all_to_all x1, waiting for transfers between devices, shards(): lax.all_to_all(dx_part, 'expert', split_axis=0, concat_axis=0, tiled=True)  71.8 us
    all_gather x1, blocking collectives, shards(): lax.all_gather(gate_w, 'dp', axis=0, tiled=True)  32.2 us
    all_gather x1, blocking collectives, shards(): lax.all_gather(down_w, 'dp', axis=0, tiled=True)  28.6 us
    all_gather x1, blocking collectives, shards(): lax.all_gather(up_w, 'dp', axis=0, tiled=True)  26.5 us
    all_to_all x1, starting transfers between devices, shards(): lax.all_to_all(spread(token_slots), 'expert', split_axis=0, concat_axis=0...  11 us
    all_to_all x2, local copies, waits for them, and re-layouts, shards(): lax.all_to_all(dx_part, 'expert', split_axis=0, concat_axis=0, tiled=True)  11 us
  transfers between devices with their start and end apart: 4, of which 2 were waited for; matrix products, arithmetic and copies ran while one was open for 4% of the time, Pallas kernels for 0%

commit v1 on v0

--- a/solution.py
+++ b/solution.py
@@ -6,6 +6,11 @@
 TOP = 8
 SLICES = 8
 CAP = 6
+
+
+def gather_over(x, name, along):
+    stack = jnp.stack([x] * lax.axis_size(name))
+    return jnp.concatenate(lax.all_to_all(stack, name, 0, 0), axis=along)
 
 
 def shards(tokens, cotangent, route_ids, route_gates, gate_w, up_w, down_w):
@@ -39,7 +44,7 @@
     w_gate, w_up, w_down = (
         lax.all_gather(gate_w, "dp", axis=0, tiled=True),
         lax.all_gather(up_w, "dp", axis=0, tiled=True),
-        lax.all_gather(down_w, "dp", axis=0, tiled=True),
+        gather_over(down_w, "dp", 0),
     )
     token_rows = lax.all_to_all(
         spread(token_slots), "expert", split_axis=0, concat_axis=0, tiled=True

time: 463 us -> 538 us (1.16)
  blocking collectives: 178 us -> 256 us
    all_to_all x0 -> x1, blocking collectives: none -> 95.7 us  [shards(): lax.all_to_all(spread(token_slots), 'expert', split_axis=0, concat_axis=0...]
    all_gather x1 -> x0, blocking collectives: 28.6 us -> none  [shards(): lax.all_gather(down_w, 'dp', axis=0, tiled=True)]
    all_gather x1, blocking collectives: 32.2 us -> 43.2 us  [shards(): lax.all_gather(gate_w, 'dp', axis=0, tiled=True)]
where the time goes in v1:
time: 538 us; the launch traced here: 536 us
  blocking collectives  256 us (48%)
  waiting for transfers between devices  156 us (29%)
  local copies, waits for them, and re-layouts  50.1 us (9%)
  matrix products  29.3 us (5%)
  starting transfers between devices  23 us (4%)
  between operations  14.4 us (3%)
  other arithmetic  7.4 us (1%)
    all_to_all x1, blocking collectives, shards(): lax.all_to_all(spread(token_slots), 'expert', split_axis=0, concat_axis=0...  95.7 us
    all_to_all x1, blocking collectives, shards(): lax.all_to_all(spread(scaled_slots), 'expert', split_axis=0, concat_axis=...  90.3 us
    all_to_all x1, waiting for transfers between devices, shards(): lax.all_to_all(out_part, 'expert', split_axis=0, concat_axis=0, tiled=True)  84.5 us
    all_to_all x1, waiting for transfers between devices, shards(): lax.all_to_all(dx_part, 'expert', split_axis=0, concat_axis=0, tiled=True)  71.8 us
    all_gather x1, blocking collectives, shards(): lax.all_gather(gate_w, 'dp', axis=0, tiled=True)  43.2 us
    all_gather x1, blocking collectives, shards(): lax.all_gather(up_w, 'dp', axis=0, tiled=True)  26.4 us
    all_to_all x2, local copies, waits for them, and re-layouts, shards(): lax.all_to_all(dx_part, 'expert', split_axis=0, concat_axis=0, tiled=True)  11 us
    all_to_all x2, local copies, waits for them, and re-layouts, shards(): lax.all_to_all(out_part, 'expert', split_axis=0, concat_axis=0, tiled=True)  10.9 us
  transfers between devices with their start and end apart: 4, of which 2 were waited for; matrix products, arithmetic and copies ran while one was open for 4% of the time, Pallas kernels for 0%

profile of v1, /device:TPU:2, one launch (start us, length us, event | category | flops | bytes accessed | tf_op | source)
XLA Modules:
  0.0 536.1 jit_solution(15645151735259346076)
XLA Ops:
  7.2 0.0 copy-start
  7.2 0.9 copy.27
  8.1 0.1 eq.76
  8.1 0.1 eq.70
  8.2 0.1 eq.83
  8.4 2.3 reduce-window.6
  10.6 0.3 slice_reduce_fusion
  10.9 0.2 reduce-window.9
  11.1 0.1 add_bitcast_fusion
  11.2 1.9 and.18
  13.2 3.4 eq.81
  16.6 2.9 convert_reduce_fusion
  19.6 0.3 convolution_convert_fusion.6
  19.8 0.1 broadcast_in_dim.17
  20.0 0.3 broadcast_in_dim.36
  20.2 0.0 copy-start.8
  20.2 95.7 %all_to_all.53 = bf16[64,6,3584]{2,1,0:T(8,128)(2,1)} all-to-all(bf16[64,6,3584]{2,1,0:T(8,128)(2,1)S(1)} %bitcast.38), channel_id=1, replica_groups=mesh['dp'=8,'expert'=64] {'expert'}, dimensions={0} | all-to-all | bytes 5505024 | tf_op jit(solution)/shard_map/all_to_all | solution.py:49
  115.9 1.0 stack.2
  116.9 10.3 %all-to-all-start.1 = ((bf16[8,448,128]{2,1,0:T(8,128)(2,1)}), bf16[8,448,128]{2,1,0:T(8,128)(2,1)}, u32[]{:S(2)}, u32[]{:S(2)}) async-start(bf16[8,448,128]{2,1,0:T(8,128)(2,1)} %stack.2), calls=%async_computation.1 | async-start | bytes 1835008 | tf_op jit(solution)/shard_map/all_to_all | solution.py:13
  127.3 43.2 %all_gather.6 = bf16[3584,128]{1,0:T(8,128)(2,1)S(1)} all-gather(bf16[448,128]{1,0:T(8,128)(2,1)S(1)} %copy-done.9), channel_id=1, replica_groups=mesh['dp'=8,'expert'=64] {'dp'}, dimensions={0}, use_global_device_ids=true | all-gather | bytes 1032192 | tf_op jit(solution)/shard_map/all_gather | solution.py:45
  170.5 26.4 %all_gather.7 = bf16[3584,128]{1,0:T(8,128)(2,1)S(1)} all-gather(bf16[448,128]{1,0:T(8,128)(2,1)S(1)} %copy-done.10), channel_id=1, replica_groups=mesh['dp'=8,'expert'=64] {'dp'}, dimensions={0}, use_global_device_ids=true | all-gather | bytes 1032192 | tf_op jit(solution)/shard_map/all_gather | solution.py:46
  196.9 5.8 %all_to_all.37 = bf16[384,3584]{1,0:T(8,128)(2,1)} reshape(bf16[64,6,3584]{2,1,0:T(8,128)(2,1)} %all_to_all.53) | data formatting | bytes 5505024 | tf_op jit(solution)/shard_map/all_to_all | solution.py:49
  202.7 2.8 fusion.12
  205.5 0.9 multiply_convert_fusion.2
  206.4 3.6 convolution_convert_fusion
  210.0 5.4 %all_to_all.39 = bf16[64,6,3584]{2,1,0:T(8,128)(2,1)} reshape(bf16[384,3584]{1,0:T(8,128)(2,1)} %convolution_convert_fusion) | data formatting | bytes 5505024 | tf_op jit(solution)/shard_map/all_to_all | solution.py:61
  215.4 7.0 %all-to-all-start.2 = ((bf16[64,6,3584]{2,1,0:T(8,128)(2,1)}), bf16[64,6,3584]{2,1,0:T(8,128)(2,1)}, u32[]{:S(2)}, u32[]{:S(2)}) async-start(bf16[64,6,3584]{2,1,0:T(8,128)(2,1)} %all_to_all.39), calls=%async_computation.2 | async-start | bytes 7340032 | tf_op jit(solution)/shard_map/all_to_all | solution.py:61
  222.5 0.1 copy.29
  222.6 0.1 mul.65
  222.7 0.1 copy.30
  222.9 84.5 %all-to-all-done.2 = bf16[64,6,3584]{2,1,0:T(8,128)(2,1)} async-done(((bf16[64,6,3584]{2,1,0:T(8,128)(2,1)}), bf16[64,6,3584]{2,1,0:T(8,128)(2,1)}, u32[]{:S(2)}, u32[]{:S(2)}) %all-to-all-start.2) | async-done | bytes 2752544 | tf_op jit(solution)/shard_map/all_to_all | solution.py:61
  307.4 5.5 %all_to_all.41 = bf16[384,3584]{1,0:T(8,128)(2,1)} reshape(bf16[64,6,3584]{2,1,0:T(8,128)(2,1)} %all-to-all-done.2) | data formatting | bytes 5505024 | tf_op jit(solution)/shard_map/all_to_all | solution.py:61
  312.9 2.7 fusion.5
  315.6 0.1 reshape.145
  315.8 0.2 select_reduce_fusion
  316.0 0.1 mul.72
  316.0 0.3 fusion.4
  316.3 0.1 broadcast_in_dim.39
  316.4 0.3 broadcast_in_dim.40
  316.7 90.3 %all_to_all.54 = bf16[64,6,3584]{2,1,0:T(8,128)(2,1)} all-to-all(bf16[64,6,3584]{2,1,0:T(8,128)(2,1)S(1)} %bitcast.39), channel_id=1, replica_groups=mesh['dp'=8,'expert'=64] {'expert'}, dimensions={0} | all-to-all | bytes 5505024 | tf_op jit(solution)/shard_map/all_to_all | solution.py:62
  407.0 5.5 %all_to_all.44 = bf16[384,3584]{1,0:T(8,128)(2,1)} reshape(bf16[64,6,3584]{2,1,0:T(8,128)(2,1)} %all_to_all.54) | data formatting | bytes 5505024 | tf_op jit(solution)/shard_map/all_to_all | solution.py:62
  412.5 2.6 convolution_convert_fusion.1
  415.1 2.2 multiply_convert_fusion
  417.4 0.7 convolution_convert_fusion.3
  418.1 0.9 fusion.14
  418.9 0.0 copy-start.6
  419.0 0.7 convolution_convert_fusion.2
  419.7 0.5 copy-done.6
  420.1 2.4 fusion
  422.6 5.4 %all_to_all.45 = bf16[64,6,3584]{2,1,0:T(8,128)(2,1)} reshape(bf16[384,3584]{1,0:T(8,128)(2,1)} %fusion) | data formatting | bytes 5505024 | tf_op jit(solution)/shard_map/all_to_all | solution.py:94
  428.0 5.6 %all-to-all-start.4 = ((bf16[64,6,3584]{2,1,0:T(8,128)(2,1)}), bf16[64,6,3584]{2,1,0:T(8,128)(2,1)}, u32[]{:S(2)}, u32[]{:S(2)}) async-start(bf16[64,6,3584]{2,1,0:T(8,128)(2,1)} %all_to_all.45), calls=%async_computation.4 | async-start | bytes 7340032 | tf_op jit(solution)/shard_map/all_to_all | solution.py:94
  433.6 0.0 reduce-scatter.4.cloned.1.call-start
  433.6 1.7 pad_maximum_fusion
  435.3 4.5 copy.35
  439.8 0.0 reduce-scatter.4.cloned.1.call-update
  439.9 0.1 reshape.146
  440.0 0.7 copy.31
  440.6 0.1 subtract_convert_fusion
  440.9 2.5 fusion.13
  443.4 3.4 fusion.1
  446.8 71.8 %all-to-all-done.4 = bf16[64,6,3584]{2,1,0:T(8,128)(2,1)} async-done(((bf16[64,6,3584]{2,1,0:T(8,128)(2,1)}), bf16[64,6,3584]{2,1,0:T(8,128)(2,1)}, u32[]{:S(2)}, u32[]{:S(2)}) %all-to-all-start.4) | async-done | bytes 2752544 | tf_op jit(solution)/shard_map/all_to_all | solution.py:94
  518.5 5.6 %all_to_all.47 = bf16[384,3584]{1,0:T(8,128)(2,1)} reshape(bf16[64,6,3584]{2,1,0:T(8,128)(2,1)} %all-to-all-done.4) | data formatting | bytes 5505024 | tf_op jit(solution)/shard_map/all_to_all | solution.py:94
  524.1 3.4 convolution_convert_fusion.4
  527.5 1.7 fusion.11
  (38 shorter events, 0.4 us)
Async XLA Ops:
  7.2 305.7 %copy-start = (bf16[128,3584]{1,0:T(8,128)(2,1)S(1)}, bf16[128,3584]{1,0:T(8,128)(2,1)}, u32[]{:S(2)}) copy-start(bf16[128,3584]{1,0:T(8,128)(2,1)} %param.8) | copy-start | bytes 2752516
  16.6 2.9 copy-start.7
  20.2 95.7 %copy-start.8 = (bf16[448,128]{1,0:T(8,128)(2,1)S(1)}, bf16[448,128]{1,0:T(8,128)(2,1)}, u32[]{:S(2)}) copy-start(bf16[448,128]{1,0:T(8,128)(2,1)} %param.13) | copy-start | bytes 344068
  115.9 11.4 %copy-start.9 = (bf16[448,128]{1,0:T(8,128)(2,1)S(1)}, bf16[448,128]{1,0:T(8,128)(2,1)}, u32[]{:S(2)}) copy-start(bf16[448,128]{1,0:T(8,128)(2,1)} %param.11) | copy-start | bytes 344068
  115.9 54.6 %copy-start.10 = (bf16[448,128]{1,0:T(8,128)(2,1)S(1)}, bf16[448,128]{1,0:T(8,128)(2,1)}, u32[]{:S(2)}) copy-start(bf16[448,128]{1,0:T(8,128)(2,1)} %param.12) | copy-start | bytes 344068
  116.9 89.4 %all-to-all-start.1 = ((bf16[8,448,128]{2,1,0:T(8,128)(2,1)}), bf16[8,448,128]{2,1,0:T(8,128)(2,1)}, u32[]{:S(2)}, u32[]{:S(2)}) async-start(bf16[8,448,128]{2,1,0:T(8,128)(2,1)} %stack.2), calls=%async_computation.1 | async-start | bytes 1835008 | tf_op jit(solution)/shard_map/all_to_all | solution.py:13
  196.9 8.6 %copy-start.5 = (bf16[3584,128]{1,0:T(8,128)(2,1)}, bf16[3584,128]{1,0:T(8,128)(2,1)S(1)}, u32[]{:S(2)}) copy-start(bf16[3584,128]{1,0:T(8,128)(2,1)S(1)} %all_gather.7) | copy-start | bytes 2752516
  202.7 2.8 copy-start.2
  215.4 7.0 %copy-start.11 = (f32[128,8]{0,1:T(8,128)S(1)}, f32[128,8]{0,1:T(8,128)}, u32[]{:S(2)}) copy-start(f32[128,8]{0,1:T(8,128)} %param.10) | copy-start | bytes 12292
  215.4 91.9 %all-to-all-start.2 = ((bf16[64,6,3584]{2,1,0:T(8,128)(2,1)}), bf16[64,6,3584]{2,1,0:T(8,128)(2,1)}, u32[]{:S(2)}, u32[]{:S(2)}) async-start(bf16[64,6,3584]{2,1,0:T(8,128)(2,1)} %all_to_all.39), calls=%async_computation.2 | async-start | bytes 7340032 | tf_op jit(solution)/shard_map/all_to_all | solution.py:61
  412.5 2.6 copy-start.4
  415.1 2.2 copy-start.3
  418.9 1.2 copy-start.6
  428.0 90.6 %all-to-all-start.4 = ((bf16[64,6,3584]{2,1,0:T(8,128)(2,1)}), bf16[64,6,3584]{2,1,0:T(8,128)(2,1)}, u32[]{:S(2)}, u32[]{:S(2)}) async-start(bf16[64,6,3584]{2,1,0:T(8,128)(2,1)} %all_to_all.45), calls=%async_computation.4 | async-start | bytes 7340032 | tf_op jit(solution)/shard_map/all_to_all | solution.py:94
  433.6 93.9 %reduce-scatter.4.cloned.1.call-start = ((), (), s32[]{:S(2)}) async-start(), calls=%async_computation.6 | async-start | bytes 3096576
  518.5 10.7 %copy-start.1 = (bf16[128,3584]{1,0:T(8,128)(2,1)S(1)}, bf16[128,3584]{1,0:T(8,128)(2,1)}, u32[]{:S(2)}) copy-start(bf16[128,3584]{1,0:T(8,128)(2,1)} %param.8) | copy-start | bytes 2752516
Sparse Core Ops, SparseCore 0:
  440.0 46.8 reduce-scatter.3
